TPU v7x, 32 devices: a whole 2x2x4 slice. The times are simulated.
32 devices in a mesh: dp: 8 (over z, x), mlp: 4 (over y, core).
Axes of the slice: x: 2, y: 2, z: 4, core: 2. Of those that a mesh axis runs over, the one named last changes fastest.
Arguments:
- tokens: bfloat16 [32768, 768], P(('dp', 'mlp')), may hold values from -6 to 6
- cotangent: bfloat16 [32768, 768], P(('dp', 'mlp')), may hold values from -6 to 6
- vectors: float32 [14, 768], replicated
- vector_moments: float32 [14, 768], replicated, may hold values from 819.2 to 26214.4
- decays: float32 [2], replicated, may hold values from 0.9 to 0.98
- owner: int32 [4, 3], replicated, may hold values from 0 to 7, as said below
- master_slots: float32 [8, 4, 768, 768], P('dp', 'mlp'), as said below
- left_slots: float32 [8, 4, 768, 768], P('dp', 'mlp'), as said below
- right_slots: float32 [8, 4, 768, 768], P('dp', 'mlp'), as said below
- left_roots: float32 [8, 4, 768, 768], P('dp', 'mlp'), as said below
- right_roots: float32 [8, 4, 768, 768], P('dp', 'mlp'), as said below
- grid_height: int32 [128], P(('dp', 'mlp')), may hold values from 8 to 24, as said below
- grid_width: int32 [128], P(('dp', 'mlp')), may hold values from 8 to 24, as said below
- patch_rows: int32 [32768], P(('dp', 'mlp')), may hold values from 0 to 23, as said below
- patch_cols: int32 [32768], P(('dp', 'mlp')), may hold values from 0 to 23, as said below
- segment: int32 [32768], P(('dp', 'mlp')), may hold values from 0 to 3, as said below
Outputs:
- output: bfloat16 [32768, 768], P(('dp', 'mlp'))
- input_grad: float32 [32768, 768], P(('dp', 'mlp'))
- slot_grads: float32 [8, 4, 768, 768], P('dp', 'mlp')
- new_left: float32 [8, 4, 768, 768], P('dp', 'mlp')
- new_right: float32 [8, 4, 768, 768], P('dp', 'mlp')
- new_master: float32 [8, 4, 768, 768], P('dp', 'mlp')
- vector_grads: float32 [14, 768], P(None, 'mlp')
- new_vector_moments: float32 [14, 768], P(None, 'mlp')
- new_vectors: float32 [14, 768], P(None, 'mlp')
Inputs may be any that keep to these rules, and one draw needn't show every extreme that they name: `owner`: the entries of a row differ; block kind 0 of row m is the m-th of the query, key, value and output projections, kind 1 the m-th 768 columns of the up projection, kind 2 the m-th 768 rows of the down projection. `master_slots`: slot (owner[m,k], m) holds block kind k of row m; the other slots are unused. `left_slots`: symmetric and positive definite. `right_slots`: symmetric and positive definite. `left_roots`: symmetric and positive definite. `right_roots`: symmetric and positive definite. `grid_height`: each image is 16 patches along one side; the other sides of one device's images add up to 64. `grid_width`: as grid_height. `patch_rows`: each device's patches hold its images whole, one after another in the order of their numbers, each in raster order. `patch_cols`: as patch_rows. `segment`: never falls within a device's patches.
All inputs are finite; a program needn't handle non-finite values.
Results may differ from a plain program's by a relative error of at most 0.014.
Values may be sent and summed in bfloat16 or wider, within the bound.
A program may use at most 192 MiB of HBM per device.

v0:
```python
import math
import jax
import jax.numpy as jnp
from jax import lax
from jax.sharding import PartitionSpec as P

HEADS = 12
GRID_BASE = 16
NORM_EPSILON = 1e-06
GRAFT_EPSILON = 1e-06
STEP_EPSILON = 1e-08
RATE_MATRIX = 0.04
RATE_VECTOR = 0.02
MASKED_SCORE = -1e30


def layer_norm(values, gain_row, shift_row):
    centred = values - jnp.mean(values, axis=-1, keepdims=True)
    spread = jnp.mean(centred * centred, axis=-1, keepdims=True)
    return centred * lax.rsqrt(spread + NORM_EPSILON) * gain_row + shift_row


def exact_gelu(values):
    return jax.nn.gelu(values, approximate=False)


def rotate_pairs(flat_values, freq_row, rows_pos, cols_pos):
    tokens_here = flat_values.shape[0]
    values = flat_values.reshape(tokens_here, HEADS, -1)
    half_size = values.shape[-1] // 2
    middle = freq_row.shape[0] // 2
    freq_cols = freq_row[:middle].reshape(HEADS, half_size)
    freq_rows = freq_row[middle:].reshape(HEADS, half_size)
    angle_grid = (
        rows_pos[:, None, None] * freq_rows[None] + cols_pos[:, None, None] * freq_cols[None]
    )
    cosine = jnp.cos(angle_grid)
    sine_part = jnp.sin(angle_grid)
    first_half = values[..., :half_size]
    second = values[..., half_size:]
    turned = jnp.concatenate(
        [first_half * cosine - second * sine_part, second * cosine + first_half * sine_part],
        axis=-1,
    )
    return turned.reshape(tokens_here, -1)


def patch_positions(segment_ids, heights_in, widths_in, rows_in, cols_in):
    images_here = heights_in.shape[0]
    matches = segment_ids[:, None] == jnp.arange(images_here, dtype=jnp.int32)[None, :]
    heights = jnp.sum(jnp.where(matches, heights_in[None, :], 0), axis=1).astype(jnp.float32)
    widths = jnp.sum(jnp.where(matches, widths_in[None, :], 0), axis=1).astype(jnp.float32)
    rows_pos = rows_in.astype(jnp.float32) * GRID_BASE / heights
    cols_pos = cols_in.astype(jnp.float32) * GRID_BASE / widths
    return (rows_pos, cols_pos)


def heads_first(flat_values):
    return jnp.swapaxes(flat_values.reshape(flat_values.shape[0], HEADS, -1), 0, 1)


def tokens_first(stacked):
    return jnp.swapaxes(stacked, 0, 1).reshape(stacked.shape[1], -1)


def local(
    tokens,
    cotangent,
    vectors,
    vector_moments,
    decays,
    owner,
    master_slots,
    left_slots,
    right_slots,
    left_roots,
    right_roots,
    grid_height,
    grid_width,
    patch_rows,
    patch_cols,
    segment,
):
    dp_index = lax.axis_index("dp")
    mlp_index = lax.axis_index("mlp")
    groups_mlp = lax.axis_size("mlp")
    model_width = tokens.shape[1]
    rows_here = tokens.shape[0]
    owner_row = jnp.take(owner, mlp_index, axis=0)
    holds_block = owner_row == dp_index
    owned_blocks = jnp.where(holds_block[:, None, None], master_slots[0, 0][None], 0.0)
    blocks = lax.psum(owned_blocks, "dp")
    blocks_low = blocks.astype(jnp.bfloat16)
    up_rows = vectors[8 : 8 + groups_mlp]
    down_bias = vectors[8 + groups_mlp]
    freq_row = vectors[9 + groups_mlp]
    every_block = lax.all_gather(blocks_low[None], "mlp", axis=0, tiled=True)
    attention_weights = every_block[:, 0]
    up_weight = every_block[:, 1]
    down_weight = every_block[:, 2]
    up_bias = up_rows.reshape(-1)
    inputs = tokens.astype(jnp.float32)
    norm_one, norm_one_back = jax.vjp(layer_norm, inputs, vectors[0], vectors[1])
    norm_one_low = norm_one.astype(jnp.bfloat16)
    query_lin = (
        jnp.dot(norm_one_low, attention_weights[0], preferred_element_type=jnp.float32) + vectors[2]
    )
    key_lin = (
        jnp.dot(norm_one_low, attention_weights[1], preferred_element_type=jnp.float32) + vectors[3]
    )
    value_low = (
        jnp.dot(norm_one_low, attention_weights[2], preferred_element_type=jnp.float32) + vectors[4]
    ).astype(jnp.bfloat16)
    rows_pos, cols_pos = patch_positions(segment, grid_height, grid_width, patch_rows, patch_cols)

    def rotary_map(flat_values, freq_values):
        return rotate_pairs(flat_values, freq_values, rows_pos, cols_pos)

    query_rot, query_back = jax.vjp(rotary_map, query_lin, freq_row)
    key_rot, key_back = jax.vjp(rotary_map, key_lin, freq_row)
    query_heads = heads_first(query_rot.astype(jnp.bfloat16))
    key_heads = heads_first(key_rot.astype(jnp.bfloat16))
    value_heads = heads_first(value_low)
    same_image = segment[:, None] == segment[None, :]
    score_scale = 1.0 / math.sqrt(model_width // HEADS)

    def head_scores(query_head, key_head):
        scores = jnp.dot(query_head, key_head.T, preferred_element_type=jnp.float32) * score_scale
        return jnp.where(same_image, scores, MASKED_SCORE)

    def head_forward(pieces):
        query_head, key_head, value_head = pieces
        scores = head_scores(query_head, key_head)
        row_peak = jnp.max(scores, axis=1, keepdims=True)
        exponent = jnp.exp(scores - row_peak)
        row_total = jnp.sum(exponent, axis=1, keepdims=True)
        weights_low = (exponent / row_total).astype(jnp.bfloat16)
        attended = jnp.dot(weights_low, value_head, preferred_element_type=jnp.float32)
        return (attended, (row_peak + jnp.log(row_total))[:, 0])

    attended_heads, log_totals = lax.map(head_forward, (query_heads, key_heads, value_heads))
    attended_low = tokens_first(attended_heads).astype(jnp.bfloat16)
    branch_one = (
        jnp.dot(attended_low, attention_weights[3], preferred_element_type=jnp.float32) + vectors[5]
    )
    middle = inputs + branch_one
    norm_two, norm_two_back = jax.vjp(layer_norm, middle, vectors[6], vectors[7])
    norm_two_low = norm_two.astype(jnp.bfloat16)
    pre_act = (
        jnp.einsum(
            "td,mde->tme", norm_two_low, up_weight, preferred_element_type=jnp.float32
        ).reshape(rows_here, -1)
        + up_bias
    )
    activation, gelu_back = jax.vjp(exact_gelu, pre_act)
    activation_blocks = activation.astype(jnp.bfloat16).reshape(rows_here, groups_mlp, -1)
    branch_two = (
        jnp.einsum(
            "tme,med->td", activation_blocks, down_weight, preferred_element_type=jnp.float32
        )
        + down_bias
    )
    grad_act = jnp.einsum(
        "td,med->tme", cotangent, down_weight, preferred_element_type=jnp.float32
    ).reshape(rows_here, -1)
    grad_down = jnp.einsum(
        "tme,td->med", activation_blocks, cotangent, preferred_element_type=jnp.float32
    )
    grad_pre_blocks = gelu_back(grad_act)[0].astype(jnp.bfloat16).reshape(rows_here, groups_mlp, -1)
    grad_up = jnp.einsum(
        "td,tme->mde", norm_two_low, grad_pre_blocks, preferred_element_type=jnp.float32
    )
    up_grad_rows = jnp.sum(grad_pre_blocks, axis=0, dtype=jnp.float32)
    grad_norm_two = jnp.einsum(
        "tme,mde->td", grad_pre_blocks, up_weight, preferred_element_type=jnp.float32
    )
    output_low = (middle + branch_two).astype(jnp.bfloat16)
    grad_middle_norm, grad_gain_two, grad_shift_two = norm_two_back(grad_norm_two)
    grad_middle = cotangent.astype(jnp.float32) + grad_middle_norm
    grad_branch_low = grad_middle.astype(jnp.bfloat16)
    grad_out_bias = jnp.sum(grad_branch_low, axis=0, dtype=jnp.float32)
    grad_out_weight = jnp.dot(attended_low.T, grad_branch_low, preferred_element_type=jnp.float32)
    grad_attended_low = jnp.dot(
        grad_branch_low, attention_weights[3].T, preferred_element_type=jnp.float32
    ).astype(jnp.bfloat16)

    def head_backward(pieces):
        query_head, key_head, value_head, grad_head, log_total = pieces
        scores = head_scores(query_head, key_head)
        probs = jnp.exp(scores - log_total[:, None])
        grad_probs = jnp.dot(grad_head, value_head.T, preferred_element_type=jnp.float32)
        inner = jnp.sum(probs * grad_probs, axis=1, keepdims=True)
        grad_scores = (probs * (grad_probs - inner)).astype(jnp.bfloat16)
        grad_query = (
            jnp.dot(grad_scores, key_head, preferred_element_type=jnp.float32) * score_scale
        )
        grad_key = (
            jnp.dot(grad_scores.T, query_head, preferred_element_type=jnp.float32) * score_scale
        )
        grad_value = jnp.dot(
            probs.astype(jnp.bfloat16).T, grad_head, preferred_element_type=jnp.float32
        )
        return (grad_query, grad_key, grad_value)

    grad_queries, grad_keys, grad_values = lax.map(
        head_backward,
        (query_heads, key_heads, value_heads, heads_first(grad_attended_low), log_totals),
    )
    grad_query_lin, grad_freq_query = query_back(tokens_first(grad_queries))
    grad_key_lin, grad_freq_key = key_back(tokens_first(grad_keys))
    grad_query_low = grad_query_lin.astype(jnp.bfloat16)
    grad_key_low = grad_key_lin.astype(jnp.bfloat16)
    grad_value_low = tokens_first(grad_values).astype(jnp.bfloat16)
    grad_query_weight = jnp.dot(norm_one_low.T, grad_query_low, preferred_element_type=jnp.float32)
    grad_key_weight = jnp.dot(norm_one_low.T, grad_key_low, preferred_element_type=jnp.float32)
    grad_value_weight = jnp.dot(norm_one_low.T, grad_value_low, preferred_element_type=jnp.float32)
    grad_norm_one = jnp.dot(
        grad_query_low, attention_weights[0].T, preferred_element_type=jnp.float32
    )
    grad_norm_one = grad_norm_one + jnp.dot(
        grad_key_low, attention_weights[1].T, preferred_element_type=jnp.float32
    )
    grad_norm_one = grad_norm_one + jnp.dot(
        grad_value_low, attention_weights[2].T, preferred_element_type=jnp.float32
    )
    grad_input_norm, grad_gain_one, grad_shift_one = norm_one_back(grad_norm_one)
    input_grad = grad_middle + grad_input_norm
    head_rows = jnp.stack(
        [
            grad_gain_one,
            grad_shift_one,
            jnp.sum(grad_query_low, axis=0, dtype=jnp.float32),
            jnp.sum(grad_key_low, axis=0, dtype=jnp.float32),
            jnp.sum(grad_value_low, axis=0, dtype=jnp.float32),
            grad_out_bias,
            grad_gain_two,
            grad_shift_two,
        ]
    )
    tail_rows = jnp.stack(
        [jnp.sum(cotangent, axis=0, dtype=jnp.float32), grad_freq_query + grad_freq_key]
    )
    local_vectors = jnp.concatenate([head_rows, up_grad_rows, tail_rows], axis=0)
    vector_sum = lax.psum(local_vectors, ("dp", "mlp"))
    attention_grads = jnp.stack(
        [grad_query_weight, grad_key_weight, grad_value_weight, grad_out_weight]
    )
    attention_share, up_share, down_share = (
        lax.psum_scatter(
            attention_grads.astype(jnp.bfloat16), "mlp", scatter_dimension=0, tiled=True
        ).astype(jnp.float32),
        lax.psum_scatter(
            grad_up.astype(jnp.bfloat16), "mlp", scatter_dimension=0, tiled=True
        ).astype(jnp.float32),
        lax.psum_scatter(
            grad_down.astype(jnp.bfloat16), "mlp", scatter_dimension=0, tiled=True
        ).astype(jnp.float32),
    )
    grad_stack = jnp.concatenate([attention_share, up_share, down_share], axis=0)
    reduced = lax.psum(grad_stack, "dp")
    block_kind = jnp.sum(jnp.where(holds_block, jnp.arange(3, dtype=jnp.int32), 0))
    owns_block = jnp.any(holds_block)
    gradient = jnp.take(reduced, block_kind, axis=0)
    decay_matrix = decays[0]
    left_old = left_slots[0, 0]
    right_old = right_slots[0, 0]
    master_old = master_slots[0, 0]
    left_next = decay_matrix * left_old + (1.0 - decay_matrix) * jnp.dot(
        gradient, gradient.T, precision=lax.Precision.HIGHEST
    )
    right_next = decay_matrix * right_old + (1.0 - decay_matrix) * jnp.dot(
        gradient.T, gradient, precision=lax.Precision.HIGHEST
    )
    direction = jnp.dot(
        jnp.dot(left_roots[0, 0], gradient, precision=lax.Precision.HIGHEST),
        right_roots[0, 0],
        precision=lax.Precision.HIGHEST,
    )
    normed_step = direction * lax.rsqrt(jnp.mean(direction * direction) + GRAFT_EPSILON)
    master_next = master_old - RATE_MATRIX * normed_step
    slot_grad = jnp.where(owns_block, gradient, 0.0)[None, None]
    left_out = jnp.where(owns_block, left_next, left_old)[None, None]
    right_out = jnp.where(owns_block, right_next, right_old)[None, None]
    master_out = jnp.where(owns_block, master_next, master_old)[None, None]
    share_width = model_width // groups_mlp

    def own_columns(table):
        return lax.dynamic_slice_in_dim(table, mlp_index * share_width, share_width, 1)

    grad_share = own_columns(vector_sum)
    moment_old = own_columns(vector_moments)
    vector_old = own_columns(vectors)
    decay_vector = decays[1]
    moment_next = decay_vector * moment_old + (1.0 - decay_vector) * grad_share * grad_share
    vector_next = vector_old - RATE_VECTOR * grad_share / (jnp.sqrt(moment_next) + STEP_EPSILON)
    return (
        output_low,
        input_grad,
        slot_grad,
        left_out,
        right_out,
        master_out,
        grad_share,
        moment_next,
        vector_next,
    )


def solution(mesh):
    placed = (
        P(("dp", "mlp"), None),
        P(("dp", "mlp"), None),
        P(),
        P(),
        P(),
        P(),
        P("dp", "mlp", None, None),
        P("dp", "mlp", None, None),
        P("dp", "mlp", None, None),
        P("dp", "mlp", None, None),
        P("dp", "mlp", None, None),
        P(("dp", "mlp")),
        P(("dp", "mlp")),
        P(("dp", "mlp")),
        P(("dp", "mlp")),
        P(("dp", "mlp")),
    )
    return jax.shard_map(
        local,
        mesh=mesh,
        in_specs=placed,
        out_specs=(
            P(("dp", "mlp"), None),
            P(("dp", "mlp"), None),
            P("dp", "mlp", None, None),
            P("dp", "mlp", None, None),
            P("dp", "mlp", None, None),
            P("dp", "mlp", None, None),
            P(None, "mlp"),
            P(None, "mlp"),
            P(None, "mlp"),
        ),
        check_vma=False,
    )
```

profile of v0, /device:TPU:0, one launch (start us, length us, event | category | flops | bytes accessed | tf_op | source)
XLA Modules:
  0.0 1202.3 jit_solution(14143546167382789815)
XLA Ops:
  8.8 5.2 broadcast_select_fusion
  14.0 278.3 %all-reduce.12 = bf16[3,768,768]{2,1,0:T(8,128)(2,1)} all-reduce(f32[3,768,768]{2,1,0:T(8,128)} %broadcast_select_fusion), channel_id=1, replica_groups=mesh['dp'=8,'mlp'=4] {'dp'}, use_global_device_ids=true, to_apply=%region_2.3 | all-reduce | flops 1769472 | bytes 10616832 | tf_op jit(solution)/shard_map/psum | solution.py:92
  303.2 78.7 %all-gather.3.cloned.1.call-done = bf16[12,768,768]{2,1,0:T(8,128)(2,1)} async-done(((bf16[3,768,768]{2,1,0:T(8,128)(2,1)}), bf16[12,768,768]{2,1,0:T(8,128)(2,1)}) %all-gather.3.cloned.1.call-update) | async-done | bytes 14155792 | tf_op jit(solution)/shard_map/all_gather | solution.py:97
  381.8 4.9 slice_bitcast_fusion.3
  389.7 3.8 convolution_add_fusion.1
  393.6 7.7 subtract_convert_fusion
  402.5 4.1 copy.102
  409.1 4.1 copy.103
  413.2 4.5 add_convert_fusion.4
  417.7 4.1 copy.101
  421.8 85.7 %while.32 = (s32[]{:T(128)}, bf16[12,1024,64]{1,2,0:T(8,128)(2,1)}, f32[12,1024]{1,0:T(8,128)}, bf16[12,1024,64]{2,1,0:T(8,128)(2,1)}, bf16[12,1024,64]{2,1,0:T(...) while((s32[]{:T(128)}, bf16[12,1024,64]{1,2,0:T(8,128)(2,1)}, ...), condition=%wide.region_8.9_spmd.clone.clone, body=%wide.region_5.8_spmd.clone.sunk.clone | while | flops 284163072 | bytes 13695065 | solution.py:141
  424.6 3.0 fusion.195
  431.7 3.0 fusion.195
  453.2 3.0 fusion.195
  467.4 3.0 fusion.195
  496.0 3.0 fusion.195
  507.5 10.2 fusion.64
  517.7 12.7 %copy.133 = f32[1024,3072]{1,0:T(8,128)} copy(f32[1024,3072]{0,1:T(8,128)} %bitcast.277) | data formatting | bytes 25165824 | tf_op jit(solution)/shard_map/reshape | solution.py:165
  530.3 6.6 copy.105
  537.0 4.0 fusion.140
  544.0 40.9 %convert_reduce_fusion = (f32[3072]{0:T(1024)}, bf16[1024,3072]{1,0:T(8,128)(2,1)}, f32[1024,3072]{1,0:T(8,128)}, f32[1024,3072]{1,0:T(8,128)}) fusion(f32[1024,3072]{1,0:T(8,128)S(1)} %copy-done.14, f32[3072]{0:T(1024)S(1)} %add.236, bf16[3072,768]{1,0:T(8,128)(2,1)} %bitcast.289, f32[1024,768]{0,1:T(8,128)S(1)} %get-tuple-element.370, ...), kind=kOutput, calls=%fused_computation.58 | convolution fusion | flops 5071696896 | bytes 51943424 | tf_op jit(solution)/shard_map/td,mde->tme/dot_general | solution.py:150
  584.9 12.8 %multiply_convert_fusion.1 = bf16[1024,3072]{1,0:T(8,128)(2,1)} fusion(f32[1024,3072]{1,0:T(8,128)} %get-tuple-element.336, f32[1024,3072]{1,0:T(8,128)} %get-tuple-element.371, f32[3072]{0:T(1024)S(1)} %add.236), kind=kLoop, calls=%fused_computation.60 | loop fusion | flops 12582912 | bytes 31469568 | tf_op jit(solution)/shard_map/convert_element_type | solution.py:156
  597.8 8.6 copy.137
  606.4 9.0 convolution_convert_fusion
  618.0 8.8 copy.138
  626.8 9.9 fusion.141
  636.7 3.5 copy.112
  640.2 3.9 multiply_reduce_fusion.1
  647.4 4.4 convolution_convert_fusion.1
  651.8 4.1 copy.113
  655.9 10.4 convert_bitcast_fusion
  667.0 159.3 %while.33 = (s32[]{:T(128)}, f32[12,1024,64]{1,2,0:T(8,128)}, f32[12,1024,64]{1,2,0:T(8,128)}, bf16[12,1024,64]{1,2,0:T(8,128)(2,1)}, bf16[12,1024,64]{2,1,0:T(8...) while((s32[]{:T(128)}, f32[12,1024,64]{1,2,0:T(8,128)}, ...), condition=%wide.region_15.16_spmd.clone.clone, body=%wide.region_13.15_spmd.clone.sunk.clone | while | flops 681704448 | bytes 34112624 | solution.py:205
  826.3 12.0 multiply_add_fusion.1
  840.7 7.8 multiply_add_fusion
  860.6 48.4 %reduce-scatter.4.cloned.1.call-done = bf16[1,768,768]{2,1,0:T(8,128)(2,1)} async-done(((bf16[4,768,768]{2,1,0:T(8,128)(2,1)}), bf16[1,768,768]{2,1,0:T(8,128)(2,1)}) %reduce-scatter.4.cloned.1.call-update) | async-done | bytes 1179664 | tf_op jit(solution)/shard_map/reduce_scatter | solution.py:249
  909.0 5.3 maximum_convert_fusion
  919.4 10.5 fusion.75
  932.5 3.3 fusion.114
  938.6 3.1 fusion.133
  944.2 3.3 convert_reduce_fusion.2
  947.5 3.6 copy.125
  955.9 45.1 %psum.23 = f32[14,768]{1,0:T(8,128)S(1)} all-reduce(f32[14,768]{1,0:T(8,128)S(1)} %concatenate.21), channel_id=1, replica_groups=mesh['dp'=8,'mlp'=4] {'dp','mlp'}, use_global_device_ids=true, to_apply=%region_39.40 | all-reduce | flops 10752 | bytes 86016 | tf_op jit(solution)/shard_map/psum | solution.py:244
  1003.1 143.9 %all-reduce.11.cloned.1.call-done = f32[3,768,768]{2,1,0:T(8,128)} async-done(((f32[3,768,768]{2,1,0:T(8,128)}), f32[3,768,768]{2,1,0:T(8,128)}) %all-reduce.11.cloned.1.call-update) | async-done | bytes 7077904 | tf_op jit(solution)/shard_map/psum | solution.py:260
  1147.1 13.6 %fusion.79 = f32[768,768]{1,0:T(8,128)S(1)} fusion(f32[1,1,768,768]{3,2,1,0:T(8,128)} %param.29, f32[3,768,768]{2,1,0:T(8,128)} %all-reduce.11.cloned.1.call-done, s32[]{:T(128)S(6)} %select_n.95, pred[]{:T(512)S(6)} %and.13), kind=kOutput, calls=%fused_computation.124 | convolution fusion | flops 5436407808 | bytes 7077893 | tf_op jit(solution)/shard_map/dot_general | solution.py:275
  1160.7 8.7 multiply_reduce_fusion.4
  1170.1 5.0 fusion.76
  1177.5 8.9 fusion.84
  1186.4 9.2 fusion.82
  (331 shorter events, 291.6 us)
Async XLA Ops:
  7.2 1153.5 %copy-start = (f32[1,1,768,768]{3,2,1,0:T(8,128)S(1)}, f32[1,1,768,768]{3,2,1,0:T(8,128)}, u32[]{:S(2)}) copy-start(f32[1,1,768,768]{3,2,1,0:T(8,128)} %param.30) | copy-start | bytes 7077892
  7.2 374.6 %all-gather.3.cloned.1.call-start = ((), (), s32[]{:S(2)}) async-start(), calls=%async_computation.7 | async-start | bytes 17694720 | tf_op jit(solution)/shard_map/all_gather | solution.py:97
  292.3 568.3 %reduce-scatter.8.cloned.1.call-start = ((), (), s32[]{:S(2)}) async-start(), calls=%async_computation.5 | async-start | bytes 5898240 | tf_op jit(solution)/shard_map/reduce_scatter | solution.py:255
  293.7 3.8 copy-start.38
  293.7 4.0 slice-start
  293.7 4.0 copy-start.20
  293.7 4.0 copy-start.53
  293.7 4.0 copy-start.54
  294.8 8.3 copy-start.50
  294.8 8.3 copy-start.51
  297.5 96.0 %copy-start.28 = (f32[12,32]{1,0:T(8,128)}, f32[12,32]{1,0:T(8,128)S(1)}, u32[]{:S(2)}) copy-start(f32[12,32]{1,0:T(8,128)S(1)} %mul.390) | copy-start | bytes 4612
  297.6 95.9 %copy-start.30 = (f32[12,32]{1,0:T(8,128)}, f32[12,32]{1,0:T(8,128)S(1)}, u32[]{:S(2)}) copy-start(f32[12,32]{1,0:T(8,128)S(1)} %mul.385) | copy-start | bytes 4612
  298.4 114.8 %copy-start.40 = (f32[768]{0:T(1024)}, f32[768]{0:T(1024)S(1)}, u32[]{:S(2)}) copy-start(f32[768]{0:T(1024)S(1)} %get-tuple-element.290) | copy-start | bytes 9220
  298.4 114.8 %copy-start.48 = (f32[768]{0:T(1024)}, f32[768]{0:T(1024)S(1)}, u32[]{:S(2)}) copy-start(f32[768]{0:T(1024)S(1)} %get-tuple-element.289) | copy-start | bytes 9220
  300.4 112.8 %copy-start.32 = (f32[1024]{0:T(1024)}, f32[1024]{0:T(1024)S(1)}, u32[]{:S(2)}) copy-start(f32[1024]{0:T(1024)S(1)} %broadcast_multiply_fusion.1) | copy-start | bytes 12292
  302.5 110.7 %copy-start.42 = (f32[1024]{0:T(1024)}, f32[1024]{0:T(1024)S(1)}, u32[]{:S(2)}) copy-start(f32[1024]{0:T(1024)S(1)} %fusion.118) | copy-start | bytes 12292
  303.1 90.4 %copy-start.34 = (f32[1024]{0:T(1024)}, f32[1024]{0:T(1024)S(1)}, u32[]{:S(2)}) copy-start(f32[1024]{0:T(1024)S(1)} %get-tuple-element.377) | copy-start | bytes 12292
  303.1 90.4 %copy-start.36 = (f32[1024]{0:T(1024)}, f32[1024]{0:T(1024)S(1)}, u32[]{:S(2)}) copy-start(f32[1024]{0:T(1024)S(1)} %get-tuple-element.378) | copy-start | bytes 12292
  381.8 4.9 copy-start.1
  389.7 3.9 copy-start.15
  393.5 7.8 copy-start.17
  537.0 7.0 copy-start.14
  541.0 43.9 %copy-start.4 = (f32[1024,768]{0,1:T(8,128)}, f32[1024,768]{0,1:T(8,128)S(1)}, u32[]{:S(2)}) copy-start(f32[1024,768]{0,1:T(8,128)S(1)} %get-tuple-element.370) | copy-start | bytes 9437188
  615.4 245.2 %reduce-scatter.6.cloned.1.call-start = ((), (), s32[]{:S(2)}) async-start(), calls=%async_computation.4 | async-start | bytes 5898240 | tf_op jit(solution)/shard_map/reduce_scatter | solution.py:252
  640.2 3.9 copy-start.5
  640.2 4.7 copy-start.8
  647.4 4.4 copy-start.23
  666.3 242.7 %reduce-scatter.4.cloned.1.call-start = ((), (), s32[]{:S(2)}) async-start(), calls=%async_computation.3 | async-start | bytes 5898240 | tf_op jit(solution)/shard_map/reduce_scatter | solution.py:249
  667.0 159.3 %copy-start.29 = (f32[12,32]{1,0:T(8,128)S(1)}, f32[12,32]{1,0:T(8,128)}, u32[]{:S(2)}) copy-start(f32[12,32]{1,0:T(8,128)} %copy-done.28) | copy-start | bytes 4612
  667.0 159.3 %copy-start.31 = (f32[12,32]{1,0:T(8,128)S(1)}, f32[12,32]{1,0:T(8,128)}, u32[]{:S(2)}) copy-start(f32[12,32]{1,0:T(8,128)} %copy-done.30) | copy-start | bytes 4612
  667.0 159.3 %copy-start.35 = (f32[1024]{0:T(1024)S(1)}, f32[1024]{0:T(1024)}, u32[]{:S(2)}) copy-start(f32[1024]{0:T(1024)} %copy-done.34) | copy-start | bytes 12292
  667.0 159.3 %copy-start.37 = (f32[1024]{0:T(1024)S(1)}, f32[1024]{0:T(1024)}, u32[]{:S(2)}) copy-start(f32[1024]{0:T(1024)} %copy-done.36) | copy-start | bytes 12292
  826.3 12.3 %copy-start.18 = (f32[12,1024,64]{1,2,0:T(8,128)S(1)}, f32[12,1024,64]{1,2,0:T(8,128)}, u32[]{:S(2)}) copy-start(f32[12,1024,64]{1,2,0:T(8,128)} %get-tuple-element.104) | copy-start | bytes 9437188
  838.3 2.5 copy-start.16
  838.5 17.7 %copy-start.25 = (bf16[1024,12,64]{0,2,1:T(8,128)(2,1)}, bf16[1024,12,64]{0,2,1:T(8,128)(2,1)S(1)}, u32[]{:S(2)}) copy-start(bf16[1024,12,64]{0,2,1:T(8,128)(2,1)S(1)} %get-tuple-element.342) | copy-start | bytes 4718596
  850.5 4.1 copy-start.26
  850.5 2.4 copy-start.10
  850.5 2.4 copy-start.33
  860.3 286.7 %all-reduce.11.cloned.1.call-start = ((), (), s32[]{:S(2)}) async-start(), calls=%async_computation.6 | async-start | bytes 14155776 | tf_op jit(solution)/shard_map/psum | solution.py:260
  914.4 5.1 copy-start.47
  932.5 3.3 copy-start.27
  935.7 2.8 copy-start.3
  935.8 2.8 copy-start.11
  938.6 3.2 copy-start.45
  947.5 5.5 copy-start.46
  951.0 50.0 %copy-start.39 = (f32[14,768]{1,0:T(8,128)S(1)}, f32[14,768]{1,0:T(8,128)}, u32[]{:S(2)}) copy-start(f32[14,768]{1,0:T(8,128)} %param.22) | copy-start | bytes 129028
  1170.1 5.0 copy-start.19
  1177.5 8.9 copy-start.56
  (15 other events, 26.7 us)
Sparse Core Ops, SparseCore 0:
  292.4 89.3 all-gather.2
  615.5 47.9 reduce-scatter.7
  666.4 48.3 reduce-scatter.5
  860.4 48.5 reduce-scatter.3
  914.5 232.5 all-reduce.10
where the time goes:
time: 1220 us; the launch traced here: 1200 us
  matrix products  359 us (29%)
  blocking collectives  323 us (26%)
  waiting for transfers between devices  271 us (22%)
  local copies, waits for them, and re-layouts  115 us (9%)
  other arithmetic  115 us (9%)
  between operations  18.4 us (2%)
    psum x1, blocking collectives, local(): blocks = lax.psum(owned_blocks, 'dp')  278 us
    psum x1, waiting for transfers between devices, local(): reduced = lax.psum(grad_stack, 'dp')  144 us
    all_gather x1, waiting for transfers between devices, local(): every_block = lax.all_gather(blocks_low[None], 'mlp', axis=0, tiled=True)  78.7 us
    dot_general x24, matrix products, head_scores(): jnp.dot(query_head, key_head.T, preferred_element_type=jnp.float32)  52.2 us
    reduce_scatter x1, waiting for transfers between devices, local(): lax.psum_scatter(attention_grads.astype(jnp.bfloat16), 'mlp', scatter_dim...  48.4 us
    psum x1, blocking collectives, local(): vector_sum = lax.psum(local_vectors, ('dp', 'mlp'))  45.1 us
    dot_general x1, matrix products, local(): jnp.einsum('td,mde->tme', norm_two_low, up_weight, preferred_element_type...  40.9 us
    dot_general x12, matrix products, head_forward(): jnp.dot(weights_low, value_head, preferred_element_type=jnp.float32)  35.5 us
  transfers between devices with their start and end apart: 5, of which 3 were waited for; matrix products, arithmetic and copies ran while one was open for 24% of the time, Pallas kernels for 0%

commit v1 on v0

--- a/solution.py
+++ b/solution.py
@@ -89,7 +89,9 @@
     owner_row = jnp.take(owner, mlp_index, axis=0)
     holds_block = owner_row == dp_index
     owned_blocks = jnp.where(holds_block[:, None, None], master_slots[0, 0][None], 0.0)
-    blocks = lax.psum(owned_blocks, "dp")
+    blocks = owned_blocks
+    for hop in (1, 2, 4):
+        blocks = blocks + lax.ppermute(blocks, "dp", [(dev, dev ^ hop) for dev in range(8)])
     blocks_low = blocks.astype(jnp.bfloat16)
     up_rows = vectors[8 : 8 + groups_mlp]
     down_bias = vectors[8 + groups_mlp]

time: 1220 us -> 1560 us (1.28)
  waiting for transfers between devices: 271 us -> 880 us
  blocking collectives: 323 us -> 45.1 us
    ppermute x0 -> x3, waiting for transfers between devices: none -> 607 us  [local(): lax.ppermute(blocks, 'dp', [(dev, dev ^ hop) for dev in range(8)])]
    psum x1 -> x0, blocking collectives: 278 us -> none  [local(): blocks = lax.psum(owned_blocks, 'dp')]
    unnamed x121 -> x125, local copies, waits for them, and re-layouts: 33.5 us -> 35.6 us
  transfers between devices with their start and end apart: 5 -> 8, of which waited for: 3 -> 6; matrix products, arithmetic and copies ran while one was open for 24% -> 18% of each run, Pallas kernels for 0% -> 0%
where the time goes in v1:
time: 1560 us
  waiting for transfers between devices  880 us (56%)
  matrix products  359 us (23%)
  other arithmetic  127 us (8%)
  local copies, waits for them, and re-layouts  117 us (8%)
  blocking collectives  45.1 us (3%)
  between operations  18.4 us (1%)
    ppermute x3, waiting for transfers between devices, local(): lax.ppermute(blocks, 'dp', [(dev, dev ^ hop) for dev in range(8)])  607 us
    psum x1, waiting for transfers between devices, local(): reduced = lax.psum(grad_stack, 'dp')  144 us
    all_gather x1, waiting for transfers between devices, local(): every_block = lax.all_gather(blocks_low[None], 'mlp', axis=0, tiled=True)  80.6 us
    dot_general x24, matrix products, head_scores(): jnp.dot(query_head, key_head.T, preferred_element_type=jnp.float32)  52.2 us
    reduce_scatter x1, waiting for transfers between devices, local(): lax.psum_scatter(attention_grads.astype(jnp.bfloat16), 'mlp', scatter_dim...  48.4 us
    psum x1, blocking collectives, local(): vector_sum = lax.psum(local_vectors, ('dp', 'mlp'))  45.1 us
    dot_general x1, matrix products, local(): jnp.einsum('td,mde->tme', norm_two_low, up_weight, preferred_element_type...  40.9 us
    unnamed x125, local copies, waits for them, and re-layouts  35.6 us
  transfers between devices with their start and end apart: 8, of which 6 were waited for; matrix products, arithmetic and copies ran while one was open for 18% of the time, Pallas kernels for 0%

profile of v1, /device:TPU:0, one launch (start us, length us, event | category | flops | bytes accessed | tf_op | source)
XLA Modules:
  0.0 1555.9 jit_solution(6238470963558493772)
XLA Ops:
  11.2 3.0 collective-permute-start
  14.2 152.4 %collective-permute-done = f32[3,768,768]{2,1,0:T(8,128)S(1)} collective-permute-done((f32[3,768,768]{2,1,0:T(8,128)S(1)}, f32[3,768,768]{2,1,0:T(8,128)S(1)}, u32[]{:S(2)}, u32[]{:S(2)}) %collective-permute-start) | collective-permute-done | bytes 7077920 | tf_op jit(solution)/shard_map/ppermute | solution.py:94
  171.2 151.8 %collective-permute-done.1 = f32[3,768,768]{2,1,0:T(8,128)} collective-permute-done((f32[3,768,768]{2,1,0:T(8,128)S(1)}, f32[3,768,768]{2,1,0:T(8,128)}, u32[]{:S(2)}, u32[]{:S(2)}) %collective-permute-start.1) | collective-permute-done | bytes 7077920 | tf_op jit(solution)/shard_map/ppermute | solution.py:94
  323.0 9.3 fusion.161
  334.9 302.9 %collective-permute-done.2 = f32[3,768,768]{2,1,0:T(8,128)S(1)} collective-permute-done((f32[3,768,768]{2,1,0:T(8,128)}, f32[3,768,768]{2,1,0:T(8,128)S(1)}, u32[]{:S(2)}, u32[]{:S(2)}) %collective-permute-start.2) | collective-permute-done | bytes 7077920 | tf_op jit(solution)/shard_map/ppermute | solution.py:94
  637.8 5.5 add_convert_fusion.1
  654.7 80.6 %all-gather.3.cloned.1.call-done = bf16[12,768,768]{2,1,0:T(8,128)(2,1)} async-done(((bf16[3,768,768]{2,1,0:T(8,128)(2,1)}), bf16[12,768,768]{2,1,0:T(8,128)(2,1)}) %all-gather.3.cloned.1.call-update) | async-done | bytes 14155792 | tf_op jit(solution)/shard_map/all_gather | solution.py:99
  735.3 4.9 slice_bitcast_fusion.3
  743.2 3.8 convolution_add_fusion.1
  747.1 7.7 subtract_convert_fusion
  756.0 4.1 copy.102
  762.6 4.1 copy.103
  766.7 4.5 add_convert_fusion.5
  771.2 4.1 copy.101
  775.3 85.7 %while.32 = (s32[]{:T(128)}, bf16[12,1024,64]{1,2,0:T(8,128)(2,1)}, f32[12,1024]{1,0:T(8,128)}, bf16[12,1024,64]{2,1,0:T(8,128)(2,1)}, bf16[12,1024,64]{2,1,0:T(...) while((s32[]{:T(128)}, bf16[12,1024,64]{1,2,0:T(8,128)(2,1)}, ...), condition=%wide.region_7.8_spmd.clone.clone, body=%wide.region_4.7_spmd.clone.sunk.clone | while | flops 284163072 | bytes 13695065 | solution.py:143
  785.3 3.0 fusion.197
  861.0 10.2 fusion.64
  871.2 12.7 copy.133
  883.8 6.6 copy.105
  890.5 4.0 fusion.141
  897.5 40.9 %convert_reduce_fusion = (f32[3072]{0:T(1024)}, bf16[1024,3072]{1,0:T(8,128)(2,1)}, f32[1024,3072]{1,0:T(8,128)}, f32[1024,3072]{1,0:T(8,128)}) fusion(f32[1024,3072]{1,0:T(8,128)S(1)} %copy-done.16, f32[3072]{0:T(1024)S(1)} %add.246, bf16[3072,768]{1,0:T(8,128)(2,1)} %bitcast.291, f32[1024,768]{0,1:T(8,128)S(1)} %get-tuple-element.370, ...), kind=kOutput, calls=%fused_computation.58 | convolution fusion | flops 5071696896 | bytes 51943424 | tf_op jit(solution)/shard_map/td,mde->tme/dot_general | solution.py:152
  938.5 12.8 multiply_convert_fusion.1
  951.3 8.6 copy.137
  959.9 9.0 convolution_convert_fusion
  971.6 8.8 copy.138
  980.3 9.9 fusion.142
  990.2 3.5 copy.112
  993.7 3.9 multiply_reduce_fusion.1
  1000.9 4.4 convolution_convert_fusion.1
  1005.3 4.1 copy.113
  1009.4 10.4 convert_bitcast_fusion
  1020.5 159.3 %while.33 = (s32[]{:T(128)}, f32[12,1024,64]{1,2,0:T(8,128)}, f32[12,1024,64]{1,2,0:T(8,128)}, bf16[12,1024,64]{1,2,0:T(8,128)(2,1)}, bf16[12,1024,64]{2,1,0:T(8...) while((s32[]{:T(128)}, f32[12,1024,64]{1,2,0:T(8,128)}, ...), condition=%wide.region_14.15_spmd.clone.clone, body=%wide.region_12.14_spmd.clone.sunk.clone | while | flops 681704448 | bytes 34112624 | solution.py:207
  1179.8 12.0 multiply_add_fusion.1
  1194.3 7.8 multiply_add_fusion
  1214.2 48.4 %reduce-scatter.4.cloned.1.call-done = bf16[1,768,768]{2,1,0:T(8,128)(2,1)} async-done(((bf16[4,768,768]{2,1,0:T(8,128)(2,1)}), bf16[1,768,768]{2,1,0:T(8,128)(2,1)}) %reduce-scatter.4.cloned.1.call-update) | async-done | bytes 1179664 | tf_op jit(solution)/shard_map/reduce_scatter | solution.py:251
  1262.5 5.3 maximum_convert_fusion
  1272.9 10.5 fusion.75
  1286.0 3.3 fusion.115
  1292.1 3.2 fusion.134
  1297.7 3.3 convert_reduce_fusion.2
  1301.0 3.6 copy.125
  1309.4 45.1 %psum.15 = f32[14,768]{1,0:T(8,128)S(1)} all-reduce(f32[14,768]{1,0:T(8,128)S(1)} %concatenate.21), channel_id=1, replica_groups=mesh['dp'=8,'mlp'=4] {'dp','mlp'}, use_global_device_ids=true, to_apply=%region_38.39 | all-reduce | flops 10752 | bytes 86016 | tf_op jit(solution)/shard_map/psum | solution.py:246
  1356.7 143.9 %all-reduce.10.cloned.1.call-done = f32[3,768,768]{2,1,0:T(8,128)} async-done(((f32[3,768,768]{2,1,0:T(8,128)}), f32[3,768,768]{2,1,0:T(8,128)}) %all-reduce.10.cloned.1.call-update) | async-done | bytes 7077904 | tf_op jit(solution)/shard_map/psum | solution.py:262
  1500.6 13.6 fusion.79
  1514.2 8.7 multiply_reduce_fusion.4
  1523.6 5.0 fusion.76
  1531.0 8.9 fusion.84
  1539.9 9.2 fusion.82
  (343 shorter events, 313.5 us)
Async XLA Ops:
  7.2 1507.0 %copy-start = (f32[1,1,768,768]{3,2,1,0:T(8,128)S(1)}, f32[1,1,768,768]{3,2,1,0:T(8,128)}, u32[]{:S(2)}) copy-start(f32[1,1,768,768]{3,2,1,0:T(8,128)} %param.30) | copy-start | bytes 7077892
  7.2 728.1 %all-gather.3.cloned.1.call-start = ((), (), s32[]{:S(2)}) async-start(), calls=%async_computation.7 | async-start | bytes 17694720 | tf_op jit(solution)/shard_map/all_gather | solution.py:99
  8.8 157.8 %copy-start.4 = (f32[1,1,768,768]{3,2,1,0:T(8,128)S(1)}, f32[1,1,768,768]{3,2,1,0:T(8,128)}, u32[]{:S(2)}) copy-start(f32[1,1,768,768]{3,2,1,0:T(8,128)} %param.26) | copy-start | bytes 7077892
  11.2 155.4 %collective-permute-start = (f32[3,768,768]{2,1,0:T(8,128)S(1)}, f32[3,768,768]{2,1,0:T(8,128)S(1)}, u32[]{:S(2)}, u32[]{:S(2)}) collective-permute-start(f32[3,768,768]{2,1,0:T(8,128)S(1)} %broadcast_select_fusion), channel_id=1, source_target_pairs={{0,4},{4,0},{8,12},{12,8},{16,20},{20,16},{24,28},{28,24},{1,5},{5... | collective-permute-start | bytes 21233672 | tf_op jit(solution)/shard_map/ppermute | solution.py:94
  169.4 153.6 %collective-permute-start.1 = (f32[3,768,768]{2,1,0:T(8,128)S(1)}, f32[3,768,768]{2,1,0:T(8,128)}, u32[]{:S(2)}, u32[]{:S(2)}) collective-permute-start(f32[3,768,768]{2,1,0:T(8,128)S(1)} %fusion.114), channel_id=1, source_target_pairs={{0,8},{4,12},{8,0},{12,4},{16,24},{20,28},{24,16},{28,20},{1,9},{5... | collective-permute-start | bytes 21233672 | tf_op jit(solution)/shard_map/ppermute | solution.py:94
  332.4 305.5 %collective-permute-start.2 = (f32[3,768,768]{2,1,0:T(8,128)}, f32[3,768,768]{2,1,0:T(8,128)S(1)}, u32[]{:S(2)}, u32[]{:S(2)}) collective-permute-start(f32[3,768,768]{2,1,0:T(8,128)} %fusion.161), channel_id=1, source_target_pairs={{0,16},{4,20},{8,24},{12,28},{16,0},{20,4},{24,8},{28,12},{1,17},{... | collective-permute-start | bytes 21233672 | tf_op jit(solution)/shard_map/ppermute | solution.py:94
  643.3 570.8 %reduce-scatter.8.cloned.1.call-start = ((), (), s32[]{:S(2)}) async-start(), calls=%async_computation.5 | async-start | bytes 5898240 | tf_op jit(solution)/shard_map/reduce_scatter | solution.py:257
  645.3 3.8 copy-start.40
  645.3 4.0 slice-start
  645.3 4.0 copy-start.22
  645.3 4.0 copy-start.55
  645.3 4.0 copy-start.56
  646.4 8.3 copy-start.52
  646.4 8.3 copy-start.53
  649.1 97.9 %copy-start.30 = (f32[12,32]{1,0:T(8,128)}, f32[12,32]{1,0:T(8,128)S(1)}, u32[]{:S(2)}) copy-start(f32[12,32]{1,0:T(8,128)S(1)} %mul.390) | copy-start | bytes 4612
  649.2 97.8 %copy-start.32 = (f32[12,32]{1,0:T(8,128)}, f32[12,32]{1,0:T(8,128)S(1)}, u32[]{:S(2)}) copy-start(f32[12,32]{1,0:T(8,128)S(1)} %mul.385) | copy-start | bytes 4612
  650.0 116.7 %copy-start.42 = (f32[768]{0:T(1024)}, f32[768]{0:T(1024)S(1)}, u32[]{:S(2)}) copy-start(f32[768]{0:T(1024)S(1)} %get-tuple-element.290) | copy-start | bytes 9220
  650.0 116.7 %copy-start.50 = (f32[768]{0:T(1024)}, f32[768]{0:T(1024)S(1)}, u32[]{:S(2)}) copy-start(f32[768]{0:T(1024)S(1)} %get-tuple-element.289) | copy-start | bytes 9220
  651.9 114.8 %copy-start.34 = (f32[1024]{0:T(1024)}, f32[1024]{0:T(1024)S(1)}, u32[]{:S(2)}) copy-start(f32[1024]{0:T(1024)S(1)} %broadcast_multiply_fusion.1) | copy-start | bytes 12292
  654.1 112.6 %copy-start.44 = (f32[1024]{0:T(1024)}, f32[1024]{0:T(1024)S(1)}, u32[]{:S(2)}) copy-start(f32[1024]{0:T(1024)S(1)} %fusion.119) | copy-start | bytes 12292
  654.7 92.3 %copy-start.36 = (f32[1024]{0:T(1024)}, f32[1024]{0:T(1024)S(1)}, u32[]{:S(2)}) copy-start(f32[1024]{0:T(1024)S(1)} %get-tuple-element.377) | copy-start | bytes 12292
  654.7 92.3 %copy-start.38 = (f32[1024]{0:T(1024)}, f32[1024]{0:T(1024)S(1)}, u32[]{:S(2)}) copy-start(f32[1024]{0:T(1024)S(1)} %get-tuple-element.378) | copy-start | bytes 12292
  735.3 4.9 copy-start.1
  743.2 3.9 copy-start.17
  747.0 7.8 copy-start.19
  890.5 7.0 copy-start.16
  894.5 43.9 %copy-start.6 = (f32[1024,768]{0,1:T(8,128)}, f32[1024,768]{0,1:T(8,128)S(1)}, u32[]{:S(2)}) copy-start(f32[1024,768]{0,1:T(8,128)S(1)} %get-tuple-element.370) | copy-start | bytes 9437188
  968.9 245.2 %reduce-scatter.6.cloned.1.call-start = ((), (), s32[]{:S(2)}) async-start(), calls=%async_computation.4 | async-start | bytes 5898240 | tf_op jit(solution)/shard_map/reduce_scatter | solution.py:254
  993.7 3.9 copy-start.7
  993.7 4.7 copy-start.10
  1000.9 4.4 copy-start.25
  1019.8 242.7 %reduce-scatter.4.cloned.1.call-start = ((), (), s32[]{:S(2)}) async-start(), calls=%async_computation.3 | async-start | bytes 5898240 | tf_op jit(solution)/shard_map/reduce_scatter | solution.py:251
  1020.5 159.3 %copy-start.31 = (f32[12,32]{1,0:T(8,128)S(1)}, f32[12,32]{1,0:T(8,128)}, u32[]{:S(2)}) copy-start(f32[12,32]{1,0:T(8,128)} %copy-done.30) | copy-start | bytes 4612
  1020.5 159.3 %copy-start.33 = (f32[12,32]{1,0:T(8,128)S(1)}, f32[12,32]{1,0:T(8,128)}, u32[]{:S(2)}) copy-start(f32[12,32]{1,0:T(8,128)} %copy-done.32) | copy-start | bytes 4612
  1020.5 159.3 %copy-start.37 = (f32[1024]{0:T(1024)S(1)}, f32[1024]{0:T(1024)}, u32[]{:S(2)}) copy-start(f32[1024]{0:T(1024)} %copy-done.36) | copy-start | bytes 12292
  1020.5 159.3 %copy-start.39 = (f32[1024]{0:T(1024)S(1)}, f32[1024]{0:T(1024)}, u32[]{:S(2)}) copy-start(f32[1024]{0:T(1024)} %copy-done.38) | copy-start | bytes 12292
  1179.8 12.3 copy-start.20
  1192.0 17.7 %copy-start.27 = (bf16[1024,12,64]{0,2,1:T(8,128)(2,1)}, bf16[1024,12,64]{0,2,1:T(8,128)(2,1)S(1)}, u32[]{:S(2)}) copy-start(bf16[1024,12,64]{0,2,1:T(8,128)(2,1)S(1)} %get-tuple-element.342) | copy-start | bytes 4718596
  1204.0 4.1 copy-start.28
  1213.8 286.7 %all-reduce.10.cloned.1.call-start = ((), (), s32[]{:S(2)}) async-start(), calls=%async_computation.6 | async-start | bytes 14155776 | tf_op jit(solution)/shard_map/psum | solution.py:262
  1267.9 5.1 copy-start.49
  1286.0 3.3 copy-start.29
  1289.3 2.8 copy-start.3
  1292.1 3.2 copy-start.47
  1301.0 5.5 copy-start.48
  1304.6 50.0 %copy-start.41 = (f32[14,768]{1,0:T(8,128)S(1)}, f32[14,768]{1,0:T(8,128)}, u32[]{:S(2)}) copy-start(f32[14,768]{1,0:T(8,128)} %param.22) | copy-start | bytes 129028
  1523.6 5.0 copy-start.21
  1531.0 8.9 copy-start.58
  (20 other events, 39.7 us)
Sparse Core Ops, SparseCore 0:
  643.5 91.8 all-gather.2
  969.0 47.9 reduce-scatter.7
  1020.0 48.3 reduce-scatter.5
  1214.0 48.5 reduce-scatter.3
  1268.0 232.5 all-reduce.9
